TPU v7x, 256 devices: a whole 4x4x8 slice. The times are simulated.
256 devices in a mesh: dp: 2 (over z_hi), seq: 128 (over y, x, z_lo, core).
Axes of the slice: x: 4, y: 4, z: 8 (z_hi: 2, z_lo: 4; z = z_hi * 4 + z_lo), core: 2. Of those that a mesh axis runs over, the one named last changes fastest.
Arguments:
- signal: bfloat16 [2, 262144, 256], P('dp', 'seq'), may hold values from -6 to 6
- gating: bfloat16 [2, 262144, 256], P('dp', 'seq'), may hold values from -6 to 6
- upstream: bfloat16 [2, 262144, 256], P('dp', 'seq'), may hold values from -1.5 to 1.5
- left_factor: bfloat16 [512, 512, 512], P('seq'), may hold values from -0.25 to 0.25
- right_factor: bfloat16 [512, 512, 512], P('seq'), may hold values from -0.25 to 0.25
Outputs:
- output: bfloat16 [2, 262144, 256], P('dp', 'seq')
- grad_gating: bfloat16 [2, 262144, 256], P('dp', 'seq')
- grad_signal: bfloat16 [2, 262144, 256], P('dp', 'seq')
- grad_left: bfloat16 [512, 512, 512], P('seq')
- grad_right: bfloat16 [512, 512, 512], P('seq')
All inputs are finite; a program needn't handle non-finite values.
Results may differ from a plain program's by a relative error of at most 0.0075.
Values may be sent and summed in bfloat16 or wider, within the bound.
A program may use at most 64 MiB of HBM per device.

v0:
```python
import jax
import jax.numpy as jnp
from jax import lax
from jax.sharding import PartitionSpec as P


def sent_together(arrays, axis, split_dim, concat_dim, along):
    ends, at = ([], 0)
    for a in arrays[:-1]:
        at += a.shape[along]
        ends.append(at)
    both = jnp.concatenate(arrays, axis=along)
    return tuple(
        jnp.split(
            lax.all_to_all(both, axis, split_axis=split_dim, concat_axis=concat_dim, tiled=True),
            ends,
            axis=along,
        )
    )


def over_pieces(x, axis):
    tiles = lax.all_gather(x, axis).astype(jnp.float32)
    return tiles.sum(axis=0)


def column_forward(right_factor, by_column):
    return jnp.einsum(
        "kmi,ikd->mkd", right_factor, by_column, preferred_element_type=jnp.float32
    ).astype(jnp.bfloat16)


def column_backward(right_factor, grad_column):
    return jnp.einsum(
        "kmi,mkd->ikd", right_factor, grad_column, preferred_element_type=jnp.float32
    ).astype(jnp.bfloat16)


def shards(signal, gating, upstream, left_factor, right_factor):
    block_count = left_factor.shape[0]
    block_len = left_factor.shape[1]
    channels = signal.shape[2]
    values = signal.reshape(block_count, block_len, channels)
    gate_rows = gating.reshape(block_count, block_len, channels)
    upstream_rows = upstream.reshape(block_count, block_len, channels)
    mixed_rows = jnp.einsum(
        "ikj,ijd->ikd", left_factor, values, preferred_element_type=jnp.float32
    ).astype(jnp.bfloat16)
    grad_rows = (upstream_rows.astype(jnp.float32) * gate_rows.astype(jnp.float32)).astype(
        jnp.bfloat16
    )
    by_column, grad_column = (
        lax.all_to_all(mixed_rows, "seq", split_axis=1, concat_axis=0, tiled=True),
        lax.all_to_all(grad_rows, "seq", split_axis=1, concat_axis=0, tiled=True),
    )
    second = column_forward(right_factor, by_column)
    grad_second = column_backward(right_factor, grad_column)
    mixed_out, grad_back = sent_together((second, grad_second), "seq", 0, 1, 2)
    mixed_wide = mixed_out.astype(jnp.float32)
    output = (gate_rows.astype(jnp.float32) * mixed_wide).astype(jnp.bfloat16).reshape(signal.shape)
    grad_gate = (
        (upstream_rows.astype(jnp.float32) * mixed_wide).astype(jnp.bfloat16).reshape(signal.shape)
    )
    grad_signal = (
        jnp.einsum("ikj,ikd->ijd", left_factor, grad_back, preferred_element_type=jnp.float32)
        .astype(jnp.bfloat16)
        .reshape(signal.shape)
    )
    left_term = jnp.einsum("ikd,ijd->ikj", grad_back, values, preferred_element_type=jnp.float32)
    right_term = jnp.einsum(
        "mkd,ikd->kmi", grad_column, by_column, preferred_element_type=jnp.float32
    )
    left_sum, right_sum = (
        over_pieces(left_term.astype(jnp.bfloat16), "dp").astype(jnp.float32),
        over_pieces(right_term.astype(jnp.bfloat16), "dp").astype(jnp.float32),
    )
    grad_left = left_sum.astype(jnp.bfloat16)
    grad_right = right_sum.astype(jnp.bfloat16)
    return (output, grad_gate, grad_signal, grad_left, grad_right)


def solution(mesh):
    in_specs = (
        P("dp", "seq", None),
        P("dp", "seq", None),
        P("dp", "seq", None),
        P("seq", None, None),
        P("seq", None, None),
    )
    out_specs = (
        P("dp", "seq", None),
        P("dp", "seq", None),
        P("dp", "seq", None),
        P("seq", None, None),
        P("seq", None, None),
    )
    return jax.shard_map(shards, mesh=mesh, in_specs=in_specs, out_specs=out_specs, check_vma=False)
```

profile of v0, /device:TPU:1, one launch (start us, length us, event | category | flops | bytes accessed | tf_op | source)
XLA Modules:
  0.0 379.8 jit_solution(14072103680214955816)
XLA Ops:
  7.2 2.7 convolution_convert_fusion.5
  9.9 1.8 copy.29
  11.7 14.3 %all-to-all-start = ((bf16[4,512,256]{2,0,1:T(4,128)(2,1)}), bf16[4,512,256]{2,0,1:T(4,128)(2,1)}, u32[]{:S(2)}, u32[]{:S(2)}) async-start(bf16[4,512,256]{2,0,1:T(4,128)(2,1)} %copy.29), calls=%async_computation | async-start | bytes 2097152 | tf_op jit(solution)/shard_map/all_to_all | solution.py:53
  26.0 1.5 fusion.1
  27.5 1.8 copy.32
  29.2 25.8 %all-to-all-done = bf16[4,512,256]{2,0,1:T(4,128)(2,1)} async-done(((bf16[4,512,256]{2,0,1:T(4,128)(2,1)}), bf16[4,512,256]{2,0,1:T(4,128)(2,1)}, u32[]{:S(2)}, u32[]{:S(2)}) %all-to-all-start) | async-done | bytes 1048608 | tf_op jit(solution)/shard_map/all_to_all | solution.py:53
  55.0 7.5 %all-to-all-start.1 = ((bf16[4,512,256]{2,0,1:T(4,128)(2,1)}), bf16[4,512,256]{2,0,1:T(4,128)(2,1)}, u32[]{:S(2)}, u32[]{:S(2)}) async-start(bf16[4,512,256]{2,0,1:T(4,128)(2,1)} %copy.32), calls=%async_computation.1 | async-start | bytes 2097152 | tf_op jit(solution)/shard_map/all_to_all | solution.py:54
  62.5 1.6 copy.30
  64.2 27.5 %all-to-all-done.1 = bf16[4,512,256]{2,0,1:T(4,128)(2,1)} async-done(((bf16[4,512,256]{2,0,1:T(4,128)(2,1)}), bf16[4,512,256]{2,0,1:T(4,128)(2,1)}, u32[]{:S(2)}, u32[]{:S(2)}) %all-to-all-start.1) | async-done | bytes 1048608 | tf_op jit(solution)/shard_map/all_to_all | solution.py:54
  91.7 1.6 copy.33
  96.5 4.5 %copy.35 = bf16[512,4,512]{2,1,0:T(4,128)(2,1)} copy(bf16[512,4,512]{0,2,1:T(8,128)(2,1)} %pad_maximum_fusion) | data formatting | bytes 4194304 | tf_op jit(solution)/shard_map/concatenate | solution.py:12
  101.0 7.5 %all-to-all-start.2 = ((bf16[512,4,512]{2,1,0:T(4,128)(2,1)}), bf16[512,4,512]{2,1,0:T(4,128)(2,1)}, u32[]{:S(2)}, u32[]{:S(2)}) async-start(bf16[512,4,512]{2,1,0:T(4,128)(2,1)} %copy.35), calls=%async_computation.2 | async-start | bytes 4194304 | tf_op jit(solution)/shard_map/all_to_all | solution.py:15
  108.8 3.3 convolution_convert_fusion
  112.1 137.9 %all-to-all-done.2 = bf16[512,4,512]{2,1,0:T(4,128)(2,1)} async-done(((bf16[512,4,512]{2,1,0:T(4,128)(2,1)}), bf16[512,4,512]{2,1,0:T(4,128)(2,1)}, u32[]{:S(2)}, u32[]{:S(2)}) %all-to-all-start.2) | async-done | bytes 2097184 | tf_op jit(solution)/shard_map/all_to_all | solution.py:15
  250.0 2.8 copy.36
  252.8 2.1 fusion.10
  255.0 1.6 copy.45
  256.6 3.4 convolution_convert_fusion.1
  260.0 3.3 fusion.5
  263.3 2.3 copy.39
  265.6 3.3 fusion.2
  268.9 5.5 %reduce_sum.25 = bf16[4,512,512]{2,1,0:T(8,128)(2,1)} reduce(bf16[2,4,512,512]{3,2,1,0:T(8,128)(2,1)} %bitcast.45, bf16[]{:T(256)} %constant.3.clone.1), dimensions={0}, to_apply=%region_1.0 | reduce | flops 1048576 | bytes 6291458 | tf_op jit(solution)/shard_map/reduce_sum | solution.py:24
  274.4 93.6 %all-gather.5.cloned.1.call-done = bf16[8,512,512]{2,1,0:T(8,128)(2,1)} async-done(((bf16[4,512,512]{2,1,0:T(8,128)(2,1)}), bf16[8,512,512]{2,1,0:T(8,128)(2,1)}) %all-gather.5.cloned.1.call-update) | async-done | bytes 4194320 | tf_op jit(solution)/shard_map/all_gather | solution.py:23
  368.0 4.9 %reduce_sum.24 = bf16[4,512,512]{2,1,0:T(8,128)(2,1)} reduce(bf16[2,4,512,512]{3,2,1,0:T(8,128)(2,1)} %bitcast.46, bf16[]{:T(256)} %constant.3.clone.1), dimensions={0}, to_apply=%region_0.0 | reduce | flops 1048576 | bytes 6291458 | tf_op jit(solution)/shard_map/reduce_sum | solution.py:24
  (16 shorter events, 3.5 us)
Async XLA Ops:
  7.2 86.2 %copy-start = (bf16[4,512,512]{2,1,0:T(8,128)(2,1)S(1)}, bf16[4,512,512]{2,1,0:T(8,128)(2,1)}, u32[]{:S(2)}) copy-start(bf16[4,512,512]{2,1,0:T(8,128)(2,1)} %param.9) | copy-start | bytes 6291460
  9.9 16.1 %copy-start.2 = (bf16[1,2048,256]{2,1,0:T(8,128)(2,1)S(1)}, bf16[1,2048,256]{2,1,0:T(8,128)(2,1)}, u32[]{:S(2)}) copy-start(bf16[1,2048,256]{2,1,0:T(8,128)(2,1)} %param.7) | copy-start | bytes 3145732
  11.7 43.3 %all-to-all-start = ((bf16[4,512,256]{2,0,1:T(4,128)(2,1)}), bf16[4,512,256]{2,0,1:T(4,128)(2,1)}, u32[]{:S(2)}, u32[]{:S(2)}) async-start(bf16[4,512,256]{2,0,1:T(4,128)(2,1)} %copy.29), calls=%async_computation | async-start | bytes 2097152 | tf_op jit(solution)/shard_map/all_to_all | solution.py:53
  55.0 36.7 %all-to-all-start.1 = ((bf16[4,512,256]{2,0,1:T(4,128)(2,1)}), bf16[4,512,256]{2,0,1:T(4,128)(2,1)}, u32[]{:S(2)}, u32[]{:S(2)}) async-start(bf16[4,512,256]{2,0,1:T(4,128)(2,1)} %copy.32), calls=%async_computation.1 | async-start | bytes 2097152 | tf_op jit(solution)/shard_map/all_to_all | solution.py:54
  93.3 1.0 copy-start.1
  101.0 149.0 %all-to-all-start.2 = ((bf16[512,4,512]{2,1,0:T(4,128)(2,1)}), bf16[512,4,512]{2,1,0:T(4,128)(2,1)}, u32[]{:S(2)}, u32[]{:S(2)}) async-start(bf16[512,4,512]{2,1,0:T(4,128)(2,1)} %copy.35), calls=%async_computation.2 | async-start | bytes 4194304 | tf_op jit(solution)/shard_map/all_to_all | solution.py:15
  108.5 160.4 %all-gather.7.cloned.1.call-start = ((), (), s32[]{:S(2)}) async-start(), calls=%async_computation.4 | async-start | bytes 6291456 | tf_op jit(solution)/shard_map/all_gather | solution.py:23
  112.1 255.9 %all-gather.5.cloned.1.call-start = ((), (), s32[]{:S(2)}) async-start(), calls=%async_computation.3 | async-start | bytes 6291456 | tf_op jit(solution)/shard_map/all_gather | solution.py:23
  263.3 2.4 copy-start.3
Sparse Core Ops, SparseCore 0:
  112.2 124.3 all-gather.6
  260.1 107.8 all-gather.4
where the time goes:
time: 381 us; the launch traced here: 380 us
  waiting for transfers between devices  285 us (75%)
  starting transfers between devices  29.6 us (8%)
  local copies, waits for them, and re-layouts  20.4 us (5%)
  other arithmetic  16.7 us (4%)
  matrix products  14.2 us (4%)
  between operations  14.2 us (4%)
    all_to_all x1, waiting for transfers between devices, sent_together(): lax.all_to_all(both, axis, split_axis=split_dim, concat_axis=concat_dim,...  138 us
    all_gather x2, waiting for transfers between devices, over_pieces(): tiles = lax.all_gather(x, axis).astype(jnp.float32)  93.6 us
    all_to_all x1, waiting for transfers between devices, shards(): lax.all_to_all(grad_rows, 'seq', split_axis=1, concat_axis=0, tiled=True)  27.5 us
    all_to_all x1, waiting for transfers between devices, shards(): lax.all_to_all(mixed_rows, 'seq', split_axis=1, concat_axis=0, tiled=True)  25.8 us
    all_to_all x1, starting transfers between devices, shards(): lax.all_to_all(mixed_rows, 'seq', split_axis=1, concat_axis=0, tiled=True)  14.3 us
    reduce_sum x2, other arithmetic, over_pieces(): return tiles.sum(axis=0)  10.4 us
  transfers between devices with their start and end apart: 5, of which 4 were waited for; matrix products, arithmetic and copies ran while one was open for 9% of the time, Pallas kernels for 0%

commit v1 on v0

v1 whole, which is shorter than its diff:
```python
import jax
import jax.numpy as jnp
from jax import lax
from jax.experimental import pallas as pl
from jax.experimental.pallas import tpu as pltpu
from jax.sharding import PartitionSpec as P

MESH = pl.DeviceIdType.MESH
BF = jnp.bfloat16
F32 = jnp.float32


def position():
    zh = lax.axis_index("dp")
    q = lax.axis_index("seq")
    return zh, q // 8, q % 8


def ring_device(pos, dz, dc):
    zh, yx, zc = pos
    z = (zh * 4 + zc // 2 + dz) % 8
    c = (zc + dc) % 2
    dzc = (z % 4) * 2 + c
    return (z // 4, yx * 8 + dzc), dzc


def plane_device(pos, t):
    zh, yx, zc = pos
    y = (yx // 4 + t // 4) % 4
    x = (yx + t) % 4
    return (zh, (y * 4 + x) * 8 + zc), y * 4 + x


def remote(src, dst, send, recv, device):
    return pltpu.make_async_remote_copy(
        src_ref=src, dst_ref=dst, send_sem=send, recv_sem=recv,
        device_id=device, device_id_type=MESH,
    )


def wait_bytes(ref, sem):
    pltpu.make_async_copy(ref, ref, sem).wait()


def dot(a, b, ca, cb):
    return lax.dot_general(a, b, (((ca,), (cb,)), ((), ())), preferred_element_type=F32)


def pack_matrix():
    r = lax.broadcasted_iota(jnp.int32, (256, 256), 0)
    c = lax.broadcasted_iota(jnp.int32, (256, 256), 1)
    want = ((r // 4) % 4) * 64 + (r // 16) * 4 + r % 4
    return jnp.where(c == want, 1.0, 0.0).astype(BF)


def unpack_matrix():
    r = lax.broadcasted_iota(jnp.int32, (256, 256), 0)
    c = lax.broadcasted_iota(jnp.int32, (256, 256), 1)
    want = ((r // 4) % 16) * 16 + (r % 4) * 4 + r // 64
    return jnp.where(c == want, 1.0, 0.0).astype(BF)


def kernel(
    v_hbm, g_hbm, u_hbm, l_hbm, r_hbm,
    out_hbm, gg_hbm, gs_hbm, gl_hbm, gr_hbm,
    vals, gate, up, left, right, work,
    s2, a2, b2, s1, a1, b1, s4, a4, b4, a3, b3,
    cols, gcols, gleft, gright,
    perm, load, out_sem, xs, xr, zs, zr,
):
    pos = position()
    zh, yx, zc = pos
    other = 1 - zh
    z = zh * 4 + zc // 2

    loads = [
        pltpu.make_async_copy(src, dst, load.at[n])
        for n, (src, dst) in enumerate(
            ((u_hbm, up), (g_hbm, gate), (v_hbm, vals.at[zh]), (l_hbm, left), (r_hbm, right))
        )
    ]
    for copy in loads:
        copy.start()

    barrier = pltpu.get_barrier_semaphore()

    @pl.loop(1, 16)
    def _(t):
        pl.semaphore_signal(
            barrier, inc=1, device_id=ring_device(pos, t // 2, t % 2)[0], device_id_type=MESH
        )
        pl.semaphore_signal(
            barrier, inc=1, device_id=plane_device(pos, t)[0], device_id_type=MESH
        )

    perm[0] = pack_matrix()
    perm[1] = unpack_matrix()
    pl.semaphore_wait(barrier, 30)

    partner, _ = ring_device(pos, 4, 0)
    for n in range(4):
        remote(v_hbm.at[n], vals.at[zh, n], zs.at[0], zr.at[0], partner).start()

    def pack(src, dst):
        for b in range(8):
            rows = jnp.concatenate([src[n, pl.ds(64 * b, 64)] for n in range(4)], axis=0)
            packed = dot(perm[0], rows, 1, 0).astype(BF).reshape(2, 8, 16, 256)
            dst[2 * b] = packed[0]
            dst[2 * b + 1] = packed[1]

    def unpack(src, dst):
        for b in range(8):
            rows = jnp.concatenate(
                [src[:, 2 * b].reshape(128, 256), src[:, 2 * b + 1].reshape(128, 256)], axis=0
            )
            flat = dot(perm[1], rows, 1, 0).astype(BF).reshape(4, 64, 256)
            for n in range(4):
                dst[n, pl.ds(64 * b, 64)] = flat[n]

    def plane_send(src, dst, n):
        pltpu.make_async_copy(src.at[yx], dst.at[:, yx], xr.at[n]).start()

        @pl.loop(1, 16)
        def _(t):
            device, there = plane_device(pos, t)
            remote(src.at[there], dst.at[:, yx], xs.at[n], xr.at[n], device).start()

    def ring_send(src, dst, hops, send, recv):
        for dz, dc in hops:
            device, dzc = ring_device(pos, dz, dc)
            remote(src.at[dzc], dst.at[zc], send, recv, device).start()

    def ring_own(a, b, n, first):
        pltpu.make_async_copy(a.at[zh, zc], b.at[zh, zc], zr.at[first + zh]).start()
        ring_send(
            a.at[zh], b.at[zh], ((2, 0), (6, 0), (2, 1), (6, 1)), zs.at[n], zr.at[first + zh]
        )
        ring_send(
            a.at[zh], b.at[zh], ((1, 0), (7, 0), (1, 1), (7, 1), (0, 1)),
            zs.at[n + 1], zr.at[first + zh],
        )

    def ring_other(a, b, n, first):
        pltpu.make_async_copy(a.at[other, zc], b.at[other, zc], zr.at[first + other]).start()
        ring_send(
            a.at[other], b.at[other], ((1, 0), (7, 0), (1, 1), (7, 1), (0, 1)),
            zs.at[n + 2], zr.at[first + other],
        )

    loads[0].wait()
    loads[1].wait()

    @pl.loop(0, 4)
    def _(n):
        work[n] = (up[n].astype(F32) * gate[n].astype(F32)).astype(BF)

    pack(work, s2)
    plane_send(s2, a2, 0)

    loads[2].wait()
    loads[3].wait()

    def mix(s):
        @pl.loop(0, 4)
        def _(n):
            work[n] = dot(left[n], vals[s, n], 1, 0).astype(BF)

        pack(work, s1.at[s])

    mix(zh)
    plane_send(s1.at[zh], a1.at[zh], 1)

    wait_bytes(a2, xr.at[0])
    pltpu.make_async_copy(a2.at[zc], b2.at[zh, zc], zr.at[1 + zh]).start()
    ring_send(
        a2, b2.at[zh],
        ((4, 0), (4, 1), (3, 0), (5, 0), (3, 1), (5, 1), (2, 0), (6, 0)),
        zs.at[1], zr.at[1 + zh],
    )
    ring_send(
        a2, b2.at[zh],
        ((2, 1), (6, 1), (1, 0), (7, 0), (1, 1), (7, 1), (0, 1)),
        zs.at[2], zr.at[1 + zh],
    )
    wait_bytes(a1.at[0], xr.at[1])
    ring_own(a1, b1, 3, 3)

    wait_bytes(vals.at[0], zr.at[0])
    mix(other)
    plane_send(s1.at[other], a1.at[other], 2)
    wait_bytes(a1.at[0], xr.at[2])
    ring_other(a1, b1, 3, 3)

    loads[4].wait()

    def column_back(s, n):
        wait_bytes(b2.at[0], zr.at[1 + s])
        unpack(b2.at[s], gcols.at[s])

        @pl.loop(0, 4)
        def _(k):
            work[k] = dot(right[k], gcols[s, k], 0, 0).astype(BF)

        pack(work, s4.at[s])
        plane_send(s4.at[s], a4.at[s], n)

    column_back(zh, 3)
    column_back(other, 4)

    def column(s):
        wait_bytes(b1.at[0], zr.at[3 + s])
        unpack(b1.at[s], cols.at[s])

        @pl.loop(0, 4)
        def _(k):
            work[k] = dot(right[k], cols[s, k], 1, 0).astype(BF)

        pack(work, s1.at[s])

    wait_bytes(a4.at[0], xr.at[3])
    ring_own(a4, b4, 6, 5)
    wait_bytes(a4.at[0], xr.at[4])
    ring_other(a4, b4, 6, 5)

    wait_bytes(s1.at[0, pl.ds(0, 15)], xs.at[1])
    wait_bytes(s1.at[0, pl.ds(0, 15)], xs.at[2])
    column(zh)
    column(other)
    far = jnp.where(zc % 2 == 0, 2, 6)
    for r, dz in ((0, 0), (1, 1), (2, far), (3, 7)):
        zd = (z + dz) % 8
        s, lane = zd // 4, pl.ds((zd % 4) * 2, 2)
        pltpu.make_async_copy(s1.at[s, yx, lane], a3.at[lane, yx], xr.at[5]).start()

        @pl.loop(1, 16)
        def _(t):
            device, there = plane_device(pos, t)
            remote(s1.at[s, there, lane], a3.at[lane, yx], xs.at[5], xr.at[5], device).start()

    @pl.loop(0, 4)
    def _(k):
        gright[k] = (
            dot(gcols[0, k], cols[0, k], 1, 1) + dot(gcols[1, k], cols[1, k], 1, 1)
        ).astype(BF)

    store_right = pltpu.make_async_copy(gright, gr_hbm, out_sem.at[0])
    store_right.start()

    wait_bytes(a3, xr.at[5])
    pltpu.make_async_copy(a3.at[zc], b3.at[zc], zr.at[7]).start()
    ring_send(
        a3, b3, ((far, 0), (far, 1), (1, 0), (7, 0), (1, 1), (7, 1), (0, 1)), zs.at[9], zr.at[7]
    )

    for s in (0, 1):
        wait_bytes(b4.at[0], zr.at[5 + s])
        unpack(b4.at[s], cols.at[s])

    @pl.loop(0, 4)
    def _(n):
        work[n] = dot(left[n], cols[zh, n], 0, 0).astype(BF)
        gleft[n] = (
            dot(cols[0, n], vals[0, n], 1, 1) + dot(cols[1, n], vals[1, n], 1, 1)
        ).astype(BF)

    store_left = pltpu.make_async_copy(gleft, gl_hbm, out_sem.at[1])
    store_left.start()
    store_signal = pltpu.make_async_copy(work, gs_hbm, out_sem.at[2])
    store_signal.start()

    wait_bytes(b3, zr.at[7])
    unpack(b3, cols.at[0])

    @pl.loop(0, 4)
    def _(n):
        second = cols[0, n].astype(F32)
        gcols[0, n] = (gate[n].astype(F32) * second).astype(BF)
        gcols[1, n] = (up[n].astype(F32) * second).astype(BF)

    store_out = pltpu.make_async_copy(gcols.at[0], out_hbm, out_sem.at[3])
    store_out.start()
    store_gate = pltpu.make_async_copy(gcols.at[1], gg_hbm, out_sem.at[4])
    store_gate.start()

    wait_bytes(vals.at[0], zs.at[0])
    for n in (0, 3, 4, 5):
        wait_bytes(s1.at[0, pl.ds(0, 15)], xs.at[n])
    wait_bytes(a2, zs.at[1])
    wait_bytes(a2.at[pl.ds(0, 7)], zs.at[2])
    for n in (3, 6):
        wait_bytes(a2.at[pl.ds(0, 4)], zs.at[n])
        wait_bytes(a2.at[pl.ds(0, 5)], zs.at[n + 1])
        wait_bytes(a2.at[pl.ds(0, 5)], zs.at[n + 2])
    wait_bytes(a3.at[pl.ds(0, 7)], zs.at[9])
    for store in (store_right, store_left, store_signal, store_out, store_gate):
        store.wait()


def shards(signal, gating, upstream, left_factor, right_factor):
    rows = (4, 512, 256)
    square = (4, 512, 512)
    sent = (16, 8, 16, 256)
    held = (8, 16, 16, 256)
    hbm = pl.BlockSpec(memory_space=pl.ANY)
    shape = jax.ShapeDtypeStruct
    out = pl.pallas_call(
        kernel,
        out_shape=(shape(rows, BF),) * 3 + (shape(square, BF),) * 2,
        in_specs=[hbm] * 5,
        out_specs=(hbm,) * 5,
        scratch_shapes=[
            pltpu.VMEM((2,) + rows, BF),
            pltpu.VMEM(rows, BF),
            pltpu.VMEM(rows, BF),
            pltpu.VMEM(square, BF),
            pltpu.VMEM(square, BF),
            pltpu.VMEM(rows, BF),
            pltpu.VMEM(sent, BF),
            pltpu.VMEM(held, BF),
            pltpu.VMEM((2,) + held, BF),
            pltpu.VMEM((2,) + sent, BF),
            pltpu.VMEM((2,) + held, BF),
            pltpu.VMEM((2,) + held, BF),
            pltpu.VMEM((2,) + sent, BF),
            pltpu.VMEM((2,) + held, BF),
            pltpu.VMEM((2,) + held, BF),
            pltpu.VMEM(held, BF),
            pltpu.VMEM(held, BF),
            pltpu.VMEM((2,) + rows, BF),
            pltpu.VMEM((2,) + rows, BF),
            pltpu.VMEM(square, BF),
            pltpu.VMEM(square, BF),
            pltpu.VMEM((2, 256, 256), BF),
            pltpu.SemaphoreType.DMA((5,)),
            pltpu.SemaphoreType.DMA((5,)),
            pltpu.SemaphoreType.DMA((6,)),
            pltpu.SemaphoreType.DMA((6,)),
            pltpu.SemaphoreType.DMA((10,)),
            pltpu.SemaphoreType.DMA((8,)),
        ],
        compiler_params=pltpu.CompilerParams(
            collective_id=0, has_side_effects=True, vmem_limit_bytes=60 << 20
        ),
    )(
        signal.reshape(rows), gating.reshape(rows), upstream.reshape(rows),
        left_factor, right_factor,
    )
    return tuple(o.reshape(signal.shape) for o in out[:3]) + tuple(out[3:])


def solution(mesh):
    blocks = (P("dp", "seq", None),) * 3 + (P("seq", None, None),) * 2
    return jax.shard_map(shards, mesh=mesh, in_specs=blocks, out_specs=blocks, check_vma=False)
```

time: 381 us -> 177 us (0.46)
  waiting for transfers between devices: 285 us -> 0 us
  Pallas kernels: 0 us -> 169 us
  starting transfers between devices: 29.6 us -> 0 us
  other arithmetic: 16.7 us -> 0 us
  matrix products: 14.2 us -> 0 us
  between operations: 14.2 us -> 0.66 us
  local copies, waits for them, and re-layouts: 20.4 us -> 8.1 us
    all_to_all x3 -> x0, waiting for transfers between devices: 191 us -> none  [the longest x1 138 us: sent_together(): lax.all_to_all(both, axis, split_axis=split_dim, concat_axis=concat_dim,...]
    pallas_call x0 -> x1, Pallas kernels: none -> 169 us  [shards(): pl.pallas_call(kernel, out_shape=(shape(rows, BF),) * 3 + (shape(square,...]
    all_gather x2 -> x0, waiting for transfers between devices: 93.6 us -> none  [over_pieces(): tiles = lax.all_gather(x, axis).astype(jnp.float32)]
    all_to_all x3 -> x0, starting transfers between devices: 29.3 us -> none  [the longest x1 14.3 us: shards(): lax.all_to_all(mixed_rows, 'seq', split_axis=1, concat_axis=0, tiled=True)]
    dot_general x6 -> x0, matrix products: 14.2 us -> none  [the longest x1 3.38 us: shards(): jnp.einsum('ikd,ijd->ikj', grad_back, values, preferred_element_type=jnp....]
    reduce_sum x2 -> x0, other arithmetic: 10.4 us -> none  [over_pieces(): return tiles.sum(axis=0)]
    unnamed x9 -> x13, local copies, waits for them, and re-layouts: 1.78 us -> 8.1 us
    all_to_all x3 -> x0, local copies, waits for them, and re-layouts: 6.08 us -> none  [the longest x1 2.81 us: sent_together(): lax.all_to_all(both, axis, split_axis=split_dim, concat_axis=concat_dim,...]
  transfers between devices with their start and end apart: 5 -> 0, of which waited for: 4 -> 0; matrix products, arithmetic and copies ran while one was open for 9% -> 0% of each run, Pallas kernels for 0% -> 0%
where the time goes in v1:
time: 177 us
  Pallas kernels  169 us (95%)
  local copies, waits for them, and re-layouts  8.1 us (5%)
    pallas_call x1, Pallas kernels, shards(): pl.pallas_call(kernel, out_shape=(shape(rows, BF),) * 3 + (shape(square,...  169 us
    unnamed x13, local copies, waits for them, and re-layouts  8.1 us

profile of v1, /device:TPU:1, one launch (start us, length us, event | category | flops | bytes accessed | tf_op | source)
XLA Modules:
  0.0 177.3 jit_solution(4404735160737913522)
XLA Ops:
  0.6 168.5 %shard_map.92 = (bf16[4,512,256]{2,1,0:T(8,128)(2,1)}, bf16[4,512,256]{2,1,0:T(8,128)(2,1)}, bf16[4,512,256]{2,1,0:T(8,128)(2,1)}, bf16[4,512,512]{2,1,0:T(8,128)(2,1)}, bf16[4,512,512]{2,1,0:T(8,128)(2,1)}) custom-call(bf16[4,512,256]{2,1,0:T(8,128)(2,1)} %bitcast.6, bf16[4,512,256]{2,1,0:T(8,128)(2,1)} %bitcast.7, bf16[4,512,256]{2,1,0:T(8,128)(2,1)} %bitcast.8, ...), custom_call_target="tpu_custom_call" | custom-call | tf_op jit(solution)/shard_map/pallas_call | solution.py:306
  169.1 0.0 copy-start.3
  169.2 0.0 copy-start.2
  169.2 2.4 %copy.15 = bf16[1,2048,256]{2,1,0:T(8,128)(2,1)} copy(bf16[1,2048,256]{2,1,0:T(8,128)(2,1)} %bitcast.11) | data formatting | bytes 2097152
  171.6 0.0 copy-done.3
  171.6 0.0 copy-start.1
  171.6 1.0 copy.16
  172.5 0.0 copy-done.2
  172.6 1.0 copy.17
  173.5 0.1 copy-done.1
  173.6 0.0 copy-start
  173.6 1.3 copy.18
  174.9 1.0 copy-done
  175.9 1.3 copy.19
Async XLA Ops:
  169.1 2.4 %copy-start.3 = (bf16[4,512,256]{2,1,0:T(8,128)(2,1)S(1)}, bf16[4,512,256]{2,1,0:T(8,128)(2,1)}, u32[]{:S(2)}) copy-start(bf16[4,512,256]{2,1,0:T(8,128)(2,1)} %get-tuple-element.11) | copy-start | bytes 3145732
  169.2 3.4 %copy-start.2 = (bf16[4,512,256]{2,1,0:T(8,128)(2,1)S(1)}, bf16[4,512,256]{2,1,0:T(8,128)(2,1)}, u32[]{:S(2)}) copy-start(bf16[4,512,256]{2,1,0:T(8,128)(2,1)} %get-tuple-element.12) | copy-start | bytes 3145732
  171.6 2.0 %copy-start.1 = (bf16[4,512,512]{2,1,0:T(8,128)(2,1)S(1)}, bf16[4,512,512]{2,1,0:T(8,128)(2,1)}, u32[]{:S(2)}) copy-start(bf16[4,512,512]{2,1,0:T(8,128)(2,1)} %get-tuple-element.23) | copy-start | bytes 6291460
  173.6 2.3 %copy-start = (bf16[4,512,512]{2,1,0:T(8,128)(2,1)S(1)}, bf16[4,512,512]{2,1,0:T(8,128)(2,1)}, u32[]{:S(2)}) copy-start(bf16[4,512,512]{2,1,0:T(8,128)(2,1)} %get-tuple-element.24) | copy-start | bytes 6291460

commit v2 on v1

v2 whole, which is shorter than its diff:
```python
import jax
import jax.numpy as jnp
from jax import lax
from jax.experimental import pallas as pl
from jax.experimental.pallas import tpu as pltpu
from jax.sharding import PartitionSpec as P

MESH = pl.DeviceIdType.MESH
BF = jnp.bfloat16
F32 = jnp.float32


def position():
    zh = lax.axis_index("dp")
    q = lax.axis_index("seq")
    return zh, q // 8, q % 8


def ring_device(pos, dz, dc):
    zh, yx, zc = pos
    z = (zh * 4 + zc // 2 + dz) % 8
    c = (zc + dc) % 2
    return (z // 4, yx * 8 + (z % 4) * 2 + c), ((dz + 1) % 4) * 2 + c


def plane_device(pos, t):
    zh, yx, zc = pos
    y = (yx // 4 + t // 4) % 4
    x = (yx + t) % 4
    return (zh, (y * 4 + x) * 8 + zc), y * 4 + x


def remote(src, dst, send, recv, device):
    return pltpu.make_async_remote_copy(
        src_ref=src, dst_ref=dst, send_sem=send, recv_sem=recv,
        device_id=device, device_id_type=MESH,
    )


def wait_bytes(ref, sem):
    pltpu.make_async_copy(ref, ref, sem).wait()


def dot(a, b, ca, cb):
    return lax.dot_general(a, b, (((ca,), (cb,)), ((), ())), preferred_element_type=F32)


def pack_matrix():
    r = lax.broadcasted_iota(jnp.int32, (256, 256), 0)
    c = lax.broadcasted_iota(jnp.int32, (256, 256), 1)
    want = ((r // 4) % 4) * 64 + (r // 16) * 4 + r % 4
    return jnp.where(c == want, 1.0, 0.0).astype(BF)


def unpack_matrix():
    r = lax.broadcasted_iota(jnp.int32, (256, 256), 0)
    c = lax.broadcasted_iota(jnp.int32, (256, 256), 1)
    want = ((r // 4) % 16) * 16 + (r % 4) * 4 + r // 64
    return jnp.where(c == want, 1.0, 0.0).astype(BF)


def unpack(perm, src, dst):
    for b in range(8):
        rows = jnp.concatenate(
            [src[:, 2 * b].reshape(128, 256), src[:, 2 * b + 1].reshape(128, 256)], axis=0
        )
        flat = dot(perm[1], rows, 1, 0).astype(BF).reshape(4, 64, 256)
        for n in range(4):
            dst[n, pl.ds(64 * b, 64)] = flat[n]


def kernel(
    v_hbm, g_hbm, u_hbm, l_hbm, r_hbm,
    b3, perm, gate, up, gsignal, gleft, gright,
    vals, left, right, work,
    s2, a2, b2, s1, a1, b1, s4, a4, b4, a3,
    cols, gcols, load, xs, xr, zs, zr,
):
    pos = position()
    zh, yx, zc = pos
    other = 1 - zh
    z = zh * 4 + zc // 2
    here = 2 + zc % 2
    lanes = [((j - zc // 2 + 5) % 4) * 2 for j in range(4)]

    loads = [
        pltpu.make_async_copy(src, dst, load.at[n])
        for n, (src, dst) in enumerate(
            ((u_hbm, up), (g_hbm, gate), (v_hbm, vals.at[zh]), (l_hbm, left), (r_hbm, right))
        )
    ]
    for copy in loads:
        copy.start()

    barrier = pltpu.get_barrier_semaphore()

    for dz in (4, 3, 5, 2, 6, 1, 7):
        for dc in (0, 1):
            pl.semaphore_signal(
                barrier, inc=1, device_id=ring_device(pos, dz, dc)[0], device_id_type=MESH
            )
    for t in (10, 11, 14, 9, 6, 2, 8, 15, 13, 7, 5, 12, 3, 4, 1):
        pl.semaphore_signal(barrier, inc=1, device_id=plane_device(pos, t)[0], device_id_type=MESH)
    pl.semaphore_signal(barrier, inc=1, device_id=ring_device(pos, 0, 1)[0], device_id_type=MESH)

    perm[0] = pack_matrix()
    perm[1] = unpack_matrix()
    def pack(src, dst):
        for b in range(8):
            rows = jnp.concatenate([src[n, pl.ds(64 * b, 64)] for n in range(4)], axis=0)
            packed = dot(perm[0], rows, 1, 0).astype(BF).reshape(2, 4, 2, 16, 256)
            for h in range(2):
                for j in range(4):
                    dst[2 * b + h, pl.ds(lanes[j], 2)] = packed[h, j]

    def plane_send(src, dst, n, width=8):
        lane = pl.ds(0, width)
        pltpu.make_async_copy(src.at[yx, lane], dst.at[lane, yx], xr.at[n]).start()

        @pl.loop(1, 16)
        def _(t):
            device, there = plane_device(pos, t)
            remote(src.at[there, lane], dst.at[lane, yx], xs.at[n], xr.at[n], device).start()

    def ring_send(src, dst, hops, send, recv):
        for dz, dc in hops:
            device, lane = ring_device(pos, dz, dc)
            remote(src.at[lane], dst.at[zc], send, recv, device).start()

    def ring_own(a, b, n, first):
        pltpu.make_async_copy(a.at[zh, here], b.at[zh, zc], zr.at[first + zh]).start()
        ring_send(
            a.at[zh], b.at[zh], ((2, 0), (6, 0), (2, 1), (6, 1)), zs.at[n], zr.at[first + zh]
        )
        ring_send(
            a.at[zh], b.at[zh], ((1, 0), (7, 0), (1, 1), (7, 1), (0, 1)),
            zs.at[n + 1], zr.at[first + zh],
        )

    def ring_other(a, b, n, first):
        pltpu.make_async_copy(a.at[other, here], b.at[other, zc], zr.at[first + other]).start()
        ring_send(
            a.at[other], b.at[other], ((1, 0), (7, 0), (1, 1), (7, 1), (0, 1)),
            zs.at[n + 2], zr.at[first + other],
        )

    def mix(s):
        @pl.loop(0, 4)
        def _(n):
            work[n] = dot(left[n], vals[s, n], 1, 0).astype(BF)

        pack(work, s1.at[s])

    def column_back(s):
        unpack(perm, b2.at[s], gcols.at[s])

        @pl.loop(0, 4)
        def _(k):
            work[k] = dot(right[k], gcols[s, k], 0, 0).astype(BF)

        pack(work, s4.at[s])

    def column(s):
        wait_bytes(b1.at[0], zr.at[3 + s])
        unpack(perm, b1.at[s], cols.at[s])

        @pl.loop(0, 4)
        def _(k):
            work[k] = dot(right[k], cols[s, k], 1, 0).astype(BF)

        pack(work, s1.at[s])

    loads[0].wait()
    loads[1].wait()

    @pl.loop(0, 4)
    def _(n):
        work[n] = (up[n].astype(F32) * gate[n].astype(F32)).astype(BF)

    pack(work, s2)
    pl.semaphore_wait(barrier, 30)
    partner, _ = ring_device(pos, 4, 0)

    def share_signal(first, last):
        for n in range(first, last):
            remote(v_hbm.at[n], vals.at[zh, n], zs.at[0], zr.at[0], partner).start()

    share_signal(0, 2)
    plane_send(s2, a2, 0)

    loads[2].wait()
    loads[3].wait()
    mix(zh)
    plane_send(s1.at[zh], a1.at[zh], 1)

    wait_bytes(a2, xr.at[0])
    pltpu.make_async_copy(a2.at[here], b2.at[zh, zc], zr.at[1 + zh]).start()
    ring_send(
        a2, b2.at[zh],
        ((4, 0), (4, 1), (3, 0), (5, 0), (3, 1), (5, 1), (2, 0), (6, 0)),
        zs.at[1], zr.at[1 + zh],
    )
    ring_send(
        a2, b2.at[zh],
        ((2, 1), (6, 1), (1, 0), (7, 0), (1, 1), (7, 1), (0, 1)),
        zs.at[2], zr.at[1 + zh],
    )
    share_signal(2, 4)
    wait_bytes(a1.at[0], xr.at[1])
    ring_own(a1, b1, 3, 3)

    loads[4].wait()
    wait_bytes(b2.at[0], zr.at[1 + zh])
    column_back(zh)
    plane_send(s4.at[zh], a4.at[zh], 3)
    wait_bytes(b2.at[0], zr.at[1 + other])
    column_back(other)
    plane_send(s4.at[other], a4.at[other], 4, 6)

    wait_bytes(vals.at[0], zr.at[0])
    mix(other)
    plane_send(s1.at[other], a1.at[other], 2, 6)
    wait_bytes(a1.at[0, pl.ds(0, 6)], xr.at[2])
    ring_other(a1, b1, 3, 3)
    wait_bytes(a4.at[0], xr.at[3])
    ring_own(a4, b4, 6, 5)
    wait_bytes(a4.at[0, pl.ds(0, 6)], xr.at[4])
    ring_other(a4, b4, 6, 5)

    wait_bytes(s1.at[0, pl.ds(0, 15)], xs.at[1])
    wait_bytes(s1.at[0, pl.ds(0, 15), pl.ds(0, 6)], xs.at[2])
    wait_bytes(s1.at[0, pl.ds(0, 15)], xs.at[0])
    column(zh)
    column(other)
    far = jnp.where(zc % 2 == 0, 2, 6)
    for p, dz in enumerate((7, 0, 1, far)):
        s = ((z + dz) % 8) // 4
        s2[:, 2 * p:2 * p + 2] = s1[s, :, 2 * p:2 * p + 2]
    plane_send(s2, a3, 5)

    @pl.loop(0, 4)
    def _(k):
        gright[k] = (
            dot(gcols[0, k], cols[0, k], 1, 1) + dot(gcols[1, k], cols[1, k], 1, 1)
        ).astype(BF)

    wait_bytes(a3, xr.at[5])
    pltpu.make_async_copy(a3.at[here], b3.at[zc], zr.at[7]).start()
    ring_send(
        a3, b3, ((far, 0), (far, 1), (1, 0), (7, 0), (1, 1), (7, 1), (0, 1)), zs.at[9], zr.at[7]
    )

    for s in (0, 1):
        wait_bytes(b4.at[0], zr.at[5 + s])
        unpack(perm, b4.at[s], cols.at[s])

    @pl.loop(0, 4)
    def _(n):
        gsignal[n] = dot(left[n], cols[zh, n], 0, 0).astype(BF)
        gleft[n] = (
            dot(cols[0, n], vals[0, n], 1, 1) + dot(cols[1, n], vals[1, n], 1, 1)
        ).astype(BF)

    wait_bytes(b3, zr.at[7])
    wait_bytes(vals.at[0], zs.at[0])
    for n in (3, 5):
        wait_bytes(s1.at[0, pl.ds(0, 15)], xs.at[n])
    wait_bytes(s1.at[0, pl.ds(0, 15), pl.ds(0, 6)], xs.at[4])
    wait_bytes(a2, zs.at[1])
    wait_bytes(a2.at[pl.ds(0, 7)], zs.at[2])
    for n in (3, 6):
        wait_bytes(a2.at[pl.ds(0, 4)], zs.at[n])
        wait_bytes(a2.at[pl.ds(0, 5)], zs.at[n + 1])
        wait_bytes(a2.at[pl.ds(0, 5)], zs.at[n + 2])
    wait_bytes(a3.at[pl.ds(0, 7)], zs.at[9])


def last_kernel(
    b3, perm, gate, up, gsignal, gleft, gright,
    out_hbm, gg_hbm, gs_hbm, gl_hbm, gr_hbm,
    second, out, ggate, sem, out_sem,
):
    copies = [
        pltpu.make_async_copy(src, dst, sem.at[n])
        for n, (src, dst) in enumerate(((gright, gr_hbm), (gleft, gl_hbm), (gsignal, gs_hbm)))
    ]
    for copy in copies:
        copy.start()
    unpack(perm, b3, second)
    for n in range(4):
        wide = second[n].astype(F32)
        out[n] = (gate[n].astype(F32) * wide).astype(BF)
        ggate[n] = (up[n].astype(F32) * wide).astype(BF)
        for k, (src, dst) in enumerate(((out, out_hbm), (ggate, gg_hbm))):
            copies.append(pltpu.make_async_copy(src.at[n], dst.at[n], out_sem.at[k, n]))
            copies[-1].start()
    for copy in copies:
        copy.wait()


def shards(signal, gating, upstream, left_factor, right_factor):
    rows = (4, 512, 256)
    square = (4, 512, 512)
    sent = (16, 8, 16, 256)
    held = (8, 16, 16, 256)
    hbm = pl.BlockSpec(memory_space=pl.ANY)
    vmem = pl.BlockSpec(memory_space=pltpu.VMEM)
    shape = jax.ShapeDtypeStruct
    last = pl.pallas_call(
        kernel,
        out_shape=(
            pltpu.VMEM(held, BF),
            pltpu.VMEM((2, 256, 256), BF),
            pltpu.VMEM(rows, BF),
            pltpu.VMEM(rows, BF),
            pltpu.VMEM(rows, BF),
            pltpu.VMEM(square, BF),
            pltpu.VMEM(square, BF),
        ),
        in_specs=[hbm] * 5,
        out_specs=(vmem,) * 7,
        scratch_shapes=[
            pltpu.VMEM((2,) + rows, BF),
            pltpu.VMEM(square, BF),
            pltpu.VMEM(square, BF),
            pltpu.VMEM(rows, BF),
            pltpu.VMEM(sent, BF),
            pltpu.VMEM(held, BF),
            pltpu.VMEM((2,) + held, BF),
            pltpu.VMEM((2,) + sent, BF),
            pltpu.VMEM((2,) + held, BF),
            pltpu.VMEM((2,) + held, BF),
            pltpu.VMEM((2,) + sent, BF),
            pltpu.VMEM((2,) + held, BF),
            pltpu.VMEM((2,) + held, BF),
            pltpu.VMEM(held, BF),
            pltpu.VMEM((2,) + rows, BF),
            pltpu.VMEM((2,) + rows, BF),
            pltpu.SemaphoreType.DMA((5,)),
            pltpu.SemaphoreType.DMA((6,)),
            pltpu.SemaphoreType.DMA((6,)),
            pltpu.SemaphoreType.DMA((10,)),
            pltpu.SemaphoreType.DMA((8,)),
        ],
        compiler_params=pltpu.CompilerParams(
            collective_id=0, has_side_effects=True, vmem_limit_bytes=46 << 20
        ),
    )(
        signal.reshape(rows), gating.reshape(rows), upstream.reshape(rows),
        left_factor, right_factor,
    )
    out = pl.pallas_call(
        last_kernel,
        out_shape=(shape(rows, BF),) * 3 + (shape(square, BF),) * 2,
        in_specs=[vmem] * 7,
        out_specs=(hbm,) * 5,
        scratch_shapes=[
            pltpu.VMEM(rows, BF),
            pltpu.VMEM(rows, BF),
            pltpu.VMEM(rows, BF),
            pltpu.SemaphoreType.DMA((3,)),
            pltpu.SemaphoreType.DMA((2, 4)),
        ],
        compiler_params=pltpu.CompilerParams(vmem_limit_bytes=8 << 20),
    )(*[pltpu.with_memory_space_constraint(o, pltpu.VMEM) for o in last])
    return tuple(o.reshape(signal.shape) for o in out[:3]) + tuple(out[3:])


def solution(mesh):
    blocks = (P("dp", "seq", None),) * 3 + (P("seq", None, None),) * 2
    return jax.shard_map(shards, mesh=mesh, in_specs=blocks, out_specs=blocks, check_vma=False)
```

time: 177 us -> 165 us (0.932)
  local copies, waits for them, and re-layouts: 8.1 us -> 0 us
  Pallas kernels: 169 us -> 164 us
    unnamed x13 -> x0, local copies, waits for them, and re-layouts: 8.1 us -> none
    pallas_call x1 -> x2, Pallas kernels: 169 us -> 164 us  [the longest x1 161 us: shards(): pl.pallas_call(kernel, out_shape=(pltpu.VMEM(held, BF), pltpu.VMEM((2, 25...]
where the time goes in v2:
time: 165 us
  Pallas kernels  164 us (99%)
    pallas_call x1, Pallas kernels, shards(): pl.pallas_call(kernel, out_shape=(pltpu.VMEM(held, BF), pltpu.VMEM((2, 25...  161 us

profile of v2, /device:TPU:1, one launch (start us, length us, event | category | flops | bytes accessed | tf_op | source)
XLA Modules:
  0.0 164.6 jit_solution(14058019603804610651)
XLA Ops:
  0.6 160.9 %shard_map.92 = (bf16[8,16,16,256]{3,2,1,0:T(8,128)(2,1)S(1)}, bf16[2,256,256]{2,1,0:T(8,128)(2,1)S(1)}, bf16[4,512,256]{2,1,0:T(8,128)(2,1)S(1)}, bf16[4,512,25...) custom-call(bf16[4,512,256]{2,1,0:T(8,128)(2,1)} %bitcast.6, ...), custom_call_target="tpu_custom_call" | custom-call | tf_op jit(solution)/shard_map/pallas_call | solution.py:309
  161.6 3.1 %shard_map.93 = (bf16[4,512,256]{2,1,0:T(8,128)(2,1)}, bf16[4,512,256]{2,1,0:T(8,128)(2,1)}, bf16[4,512,256]{2,1,0:T(8,128)(2,1)}, bf16[4,512,512]{2,1,0:T(8,128)(2,1)}, bf16[4,512,512]{2,1,0:T(8,128)(2,1)}) custom-call(bf16[8,16,16,256]{3,2,1,0:T(8,128)(2,1)S(1)} %get-tuple-element.17.b3, bf16[2,256,256]{2,1,0:T(8,128)(2,1)S(1)} %get-tuple-element.18.perm, ...), custom_call_target="tpu_custom_call" | custom-call | tf_op jit(solution)/shard_map/pallas_call | solution.py:352

commit v3 on v2

--- a/solution.py
+++ b/solution.py
@@ -72,7 +72,7 @@
 def kernel(
     v_hbm, g_hbm, u_hbm, l_hbm, r_hbm,
     b3, perm, gate, up, gsignal, gleft, gright,
-    vals, left, right, work,
+    vals, left, right, work, mixed,
     s2, a2, b2, s1, a1, b1, s4, a4, b4, a3,
     cols, gcols, load, xs, xr, zs, zr,
 ):
@@ -105,20 +105,22 @@
 
     perm[0] = pack_matrix()
     perm[1] = unpack_matrix()
-    def pack(src, dst):
+    def pack(src, dst, half=None):
         for b in range(8):
             rows = jnp.concatenate([src[n, pl.ds(64 * b, 64)] for n in range(4)], axis=0)
             packed = dot(perm[0], rows, 1, 0).astype(BF).reshape(2, 4, 2, 16, 256)
             for h in range(2):
                 for j in range(4):
-                    dst[2 * b + h, pl.ds(lanes[j], 2)] = packed[h, j]
+                    if half is None:
+                        dst[2 * b + h, pl.ds(lanes[j], 2)] = packed[h, j]
+                    else:
+                        dst[half[j], 2 * b + h, pl.ds(lanes[j], 2)] = packed[h, j]
 
     def plane_send(src, dst, n, width=8):
         lane = pl.ds(0, width)
         pltpu.make_async_copy(src.at[yx, lane], dst.at[lane, yx], xr.at[n]).start()
 
-        @pl.loop(1, 16)
-        def _(t):
+        for t in (10, 5, 15, 7, 13, 1, 4, 3, 12, 6, 9, 14, 11, 2, 8):
             device, there = plane_device(pos, t)
             remote(src.at[there, lane], dst.at[lane, yx], xs.at[n], xr.at[n], device).start()
 
@@ -127,14 +129,16 @@
             device, lane = ring_device(pos, dz, dc)
             remote(src.at[lane], dst.at[zc], send, recv, device).start()
 
-    def ring_own(a, b, n, first):
+    def ring_near(a, b, n, first):
         pltpu.make_async_copy(a.at[zh, here], b.at[zh, zc], zr.at[first + zh]).start()
-        ring_send(
-            a.at[zh], b.at[zh], ((2, 0), (6, 0), (2, 1), (6, 1)), zs.at[n], zr.at[first + zh]
-        )
         ring_send(
             a.at[zh], b.at[zh], ((1, 0), (7, 0), (1, 1), (7, 1), (0, 1)),
             zs.at[n + 1], zr.at[first + zh],
+        )
+
+    def ring_far(a, b, n, first):
+        ring_send(
+            a.at[zh], b.at[zh], ((2, 0), (6, 0), (2, 1), (6, 1)), zs.at[n], zr.at[first + zh]
         )
 
     def ring_other(a, b, n, first):
@@ -144,12 +148,10 @@
             zs.at[n + 2], zr.at[first + other],
         )
 
-    def mix(s):
-        @pl.loop(0, 4)
+    def mix(s, dst, first, last):
+        @pl.loop(first, last)
         def _(n):
-            work[n] = dot(left[n], vals[s, n], 1, 0).astype(BF)
-
-        pack(work, s1.at[s])
+            dst[n] = dot(left[n], vals[s, n], 1, 0).astype(BF)
 
     def column_back(s):
         unpack(perm, b2.at[s], gcols.at[s])
@@ -168,7 +170,7 @@
         def _(k):
             work[k] = dot(right[k], cols[s, k], 1, 0).astype(BF)
 
-        pack(work, s1.at[s])
+        pack(work, s1, [jnp.where(w == s, 0, 1) for w in wanted])
 
     loads[0].wait()
     loads[1].wait()
@@ -183,14 +185,15 @@
 
     def share_signal(first, last):
         for n in range(first, last):
-            remote(v_hbm.at[n], vals.at[zh, n], zs.at[0], zr.at[0], partner).start()
+            remote(v_hbm.at[n], vals.at[zh, n], zs.at[0], zr.at[8 * (n // 2)], partner).start()
 
     share_signal(0, 2)
     plane_send(s2, a2, 0)
 
     loads[2].wait()
     loads[3].wait()
-    mix(zh)
+    mix(zh, work, 0, 4)
+    pack(work, s1.at[zh])
     plane_send(s1.at[zh], a1.at[zh], 1)
 
     wait_bytes(a2, xr.at[0])
@@ -207,7 +210,8 @@
     )
     share_signal(2, 4)
     wait_bytes(a1.at[0], xr.at[1])
-    ring_own(a1, b1, 3, 3)
+    ring_far(a1, b1, 3, 3)
+    ring_near(a1, b1, 3, 3)
 
     loads[4].wait()
     wait_bytes(b2.at[0], zr.at[1 + zh])
@@ -217,26 +221,31 @@
     column_back(other)
     plane_send(s4.at[other], a4.at[other], 4, 6)
 
-    wait_bytes(vals.at[0], zr.at[0])
-    mix(other)
+    wait_bytes(vals.at[0, pl.ds(0, 2)], zr.at[0])
+    mix(other, mixed, 0, 2)
+    wait_bytes(vals.at[0, pl.ds(0, 2)], zr.at[8])
+    mix(other, mixed, 2, 4)
+    pack(mixed, s1.at[other])
     plane_send(s1.at[other], a1.at[other], 2, 6)
     wait_bytes(a1.at[0, pl.ds(0, 6)], xr.at[2])
     ring_other(a1, b1, 3, 3)
     wait_bytes(a4.at[0], xr.at[3])
-    ring_own(a4, b4, 6, 5)
+    ring_far(a4, b4, 6, 5)
+    ring_near(a4, b4, 6, 5)
     wait_bytes(a4.at[0, pl.ds(0, 6)], xr.at[4])
     ring_other(a4, b4, 6, 5)
 
     wait_bytes(s1.at[0, pl.ds(0, 15)], xs.at[1])
     wait_bytes(s1.at[0, pl.ds(0, 15), pl.ds(0, 6)], xs.at[2])
-    wait_bytes(s1.at[0, pl.ds(0, 15)], xs.at[0])
+    far = jnp.where(zc % 2 == 0, 2, 6)
+    wanted = []
+    for j in range(4):
+        hop = (j - zc // 2 + 4) % 4
+        hop = jnp.where(hop == 2, far, jnp.where(hop == 3, 7, hop))
+        wanted.append(((z + hop) % 8) // 4)
     column(zh)
     column(other)
-    far = jnp.where(zc % 2 == 0, 2, 6)
-    for p, dz in enumerate((7, 0, 1, far)):
-        s = ((z + dz) % 8) // 4
-        s2[:, 2 * p:2 * p + 2] = s1[s, :, 2 * p:2 * p + 2]
-    plane_send(s2, a3, 5)
+    plane_send(s1.at[0], a3, 5)
 
     @pl.loop(0, 4)
     def _(k):
@@ -263,7 +272,7 @@
 
     wait_bytes(b3, zr.at[7])
     wait_bytes(vals.at[0], zs.at[0])
-    for n in (3, 5):
+    for n in (0, 3, 5):
         wait_bytes(s1.at[0, pl.ds(0, 15)], xs.at[n])
     wait_bytes(s1.at[0, pl.ds(0, 15), pl.ds(0, 6)], xs.at[4])
     wait_bytes(a2, zs.at[1])
@@ -281,8 +290,9 @@
     second, out, ggate, sem, out_sem,
 ):
     copies = [
-        pltpu.make_async_copy(src, dst, sem.at[n])
+        pltpu.make_async_copy(src.at[k], dst.at[k], sem.at[n, k])
         for n, (src, dst) in enumerate(((gright, gr_hbm), (gleft, gl_hbm), (gsignal, gs_hbm)))
+        for k in range(4)
     ]
     for copy in copies:
         copy.start()
@@ -324,6 +334,7 @@
             pltpu.VMEM(square, BF),
             pltpu.VMEM(square, BF),
             pltpu.VMEM(rows, BF),
+            pltpu.VMEM(rows, BF),
             pltpu.VMEM(sent, BF),
             pltpu.VMEM(held, BF),
             pltpu.VMEM((2,) + held, BF),
@@ -340,7 +351,7 @@
             pltpu.SemaphoreType.DMA((6,)),
             pltpu.SemaphoreType.DMA((6,)),
             pltpu.SemaphoreType.DMA((10,)),
-            pltpu.SemaphoreType.DMA((8,)),
+            pltpu.SemaphoreType.DMA((9,)),
         ],
         compiler_params=pltpu.CompilerParams(
             collective_id=0, has_side_effects=True, vmem_limit_bytes=46 << 20
@@ -358,7 +369,7 @@
             pltpu.VMEM(rows, BF),
             pltpu.VMEM(rows, BF),
             pltpu.VMEM(rows, BF),
-            pltpu.SemaphoreType.DMA((3,)),
+            pltpu.SemaphoreType.DMA((3, 4)),
             pltpu.SemaphoreType.DMA((2, 4)),
         ],
         compiler_params=pltpu.CompilerParams(vmem_limit_bytes=8 << 20),

time: 165 us -> 164 us (level)
  no operation moved by 1% of the time
where the time goes in v3:
time: 164 us
  Pallas kernels  164 us (100%)
    pallas_call x1, Pallas kernels, shards(): pl.pallas_call(kernel, out_shape=(pltpu.VMEM(held, BF), pltpu.VMEM((2, 25...  160 us
    pallas_call x1, Pallas kernels, shards(): pl.pallas_call(last_kernel, out_shape=(shape(rows, BF),) * 3 + (shape(squ...  3.48 us

profile of v3, /device:TPU:1, one launch (start us, length us, event | category | flops | bytes accessed | tf_op | source)
XLA Modules:
  0.0 164.3 jit_solution(4815539166464958476)
XLA Ops:
  0.6 160.2 %shard_map.92 = (bf16[8,16,16,256]{3,2,1,0:T(8,128)(2,1)S(1)}, bf16[2,256,256]{2,1,0:T(8,128)(2,1)S(1)}, bf16[4,512,256]{2,1,0:T(8,128)(2,1)S(1)}, bf16[4,512,25...) custom-call(bf16[4,512,256]{2,1,0:T(8,128)(2,1)} %bitcast.6, ...), custom_call_target="tpu_custom_call" | custom-call | tf_op jit(solution)/shard_map/pallas_call | solution.py:319
  160.8 3.5 %shard_map.93 = (bf16[4,512,256]{2,1,0:T(8,128)(2,1)}, bf16[4,512,256]{2,1,0:T(8,128)(2,1)}, bf16[4,512,256]{2,1,0:T(8,128)(2,1)}, bf16[4,512,512]{2,1,0:T(8,128)(2,1)}, bf16[4,512,512]{2,1,0:T(8,128)(2,1)}) custom-call(bf16[8,16,16,256]{3,2,1,0:T(8,128)(2,1)S(1)} %get-tuple-element.17.b3, bf16[2,256,256]{2,1,0:T(8,128)(2,1)S(1)} %get-tuple-element.18.perm, ...), custom_call_target="tpu_custom_call" | custom-call | tf_op jit(solution)/shard_map/pallas_call | solution.py:363

commit v4 on v3

--- a/solution.py
+++ b/solution.py
@@ -290,9 +290,8 @@
     second, out, ggate, sem, out_sem,
 ):
     copies = [
-        pltpu.make_async_copy(src.at[k], dst.at[k], sem.at[n, k])
+        pltpu.make_async_copy(src, dst, sem.at[n])
         for n, (src, dst) in enumerate(((gright, gr_hbm), (gleft, gl_hbm), (gsignal, gs_hbm)))
-        for k in range(4)
     ]
     for copy in copies:
         copy.start()
@@ -369,7 +368,7 @@
             pltpu.VMEM(rows, BF),
             pltpu.VMEM(rows, BF),
             pltpu.VMEM(rows, BF),
-            pltpu.SemaphoreType.DMA((3, 4)),
+            pltpu.SemaphoreType.DMA((3,)),
             pltpu.SemaphoreType.DMA((2, 4)),
         ],
         compiler_params=pltpu.CompilerParams(vmem_limit_bytes=8 << 20),

time: 164 us -> 164 us (level)
  no operation moved by 1% of the time
where the time goes in v4:
time: 164 us
  Pallas kernels  163 us (99%)
    pallas_call x1, Pallas kernels, shards(): pl.pallas_call(kernel, out_shape=(pltpu.VMEM(held, BF), pltpu.VMEM((2, 25...  160 us

profile of v4, /device:TPU:1, one launch (start us, length us, event | category | flops | bytes accessed | tf_op | source)
XLA Modules:
  0.0 163.9 jit_solution(18008071876273658822)
XLA Ops:
  0.6 160.2 %shard_map.92 = (bf16[8,16,16,256]{3,2,1,0:T(8,128)(2,1)S(1)}, bf16[2,256,256]{2,1,0:T(8,128)(2,1)S(1)}, bf16[4,512,256]{2,1,0:T(8,128)(2,1)S(1)}, bf16[4,512,25...) custom-call(bf16[4,512,256]{2,1,0:T(8,128)(2,1)} %bitcast.6, ...), custom_call_target="tpu_custom_call" | custom-call | tf_op jit(solution)/shard_map/pallas_call | solution.py:318
  160.8 3.1 %shard_map.93 = (bf16[4,512,256]{2,1,0:T(8,128)(2,1)}, bf16[4,512,256]{2,1,0:T(8,128)(2,1)}, bf16[4,512,256]{2,1,0:T(8,128)(2,1)}, bf16[4,512,512]{2,1,0:T(8,128)(2,1)}, bf16[4,512,512]{2,1,0:T(8,128)(2,1)}) custom-call(bf16[8,16,16,256]{3,2,1,0:T(8,128)(2,1)S(1)} %get-tuple-element.17.b3, bf16[2,256,256]{2,1,0:T(8,128)(2,1)S(1)} %get-tuple-element.18.perm, ...), custom_call_target="tpu_custom_call" | custom-call | tf_op jit(solution)/shard_map/pallas_call | solution.py:362
